TPU v7x, 32 devices: a whole 2x2x4 slice. The times are simulated.
32 devices in a mesh: rep: 8 (over z, core), shard: 4 (over y, x).
Axes of the slice: x: 2, y: 2, z: 4, core: 2. Of those that a mesh axis runs over, the one named last changes fastest.
Arguments:
- tokens: bfloat16 [16384, 768], P(('rep', 'shard')), may hold values from -6 to 6
- cotangent: bfloat16 [16384, 768], P(('rep', 'shard')), may hold values from -6 to 6
- segment_ids: int32 [32, 512], P(('rep', 'shard')), may hold values from 0 to 5, never falling along the last dimension, each value on 1 to 256 neighbouring positions
- send_order: int32 [32, 512], P(('rep', 'shard')), may hold values from 0 to 511, each once within a row
- pack_order: int32 [32, 512], P(('rep', 'shard')), may hold values from 0 to 511, each once within a row
- query_weight: bfloat16 [768, 768], P('shard'), may hold values from -0.21875 to 0.21875
- key_weight: bfloat16 [768, 768], P('shard'), may hold values from -0.21875 to 0.21875
- value_weight: bfloat16 [768, 768], P('shard'), may hold values from -0.21875 to 0.21875
- out_weight: bfloat16 [768, 768], P('shard'), may hold values from -0.875 to 0.875
- up_weight: bfloat16 [768, 3072], P('shard'), may hold values from -0.21875 to 0.21875
- down_weight: bfloat16 [3072, 768], P('shard'), may hold values from -0.109375 to 0.109375
- query_bias: bfloat16 [768], P('shard'), may hold values from -3 to 3
- value_bias: bfloat16 [768], P('shard'), may hold values from -3 to 3
- out_bias: bfloat16 [768], P('shard'), may hold values from -3 to 3
- up_bias: bfloat16 [3072], P('shard'), may hold values from -3 to 3
- down_bias: bfloat16 [768], P('shard'), may hold values from -3 to 3
- first_gain: bfloat16 [768], P('shard'), may hold values from 0.5 to 1.5
- first_shift: bfloat16 [768], P('shard'), may hold values from -3 to 3
- second_gain: bfloat16 [768], P('shard'), may hold values from 0.5 to 1.5
- second_shift: bfloat16 [768], P('shard'), may hold values from -3 to 3
Outputs:
- layer_out: bfloat16 [16384, 768], P(('rep', 'shard'))
- grad_tokens: bfloat16 [16384, 768], P(('rep', 'shard'))
- grad_query_weight: float32 [768, 768], P('shard')
- grad_key_weight: float32 [768, 768], P('shard')
- grad_value_weight: float32 [768, 768], P('shard')
- grad_out_weight: float32 [768, 768], P('shard')
- grad_up_weight: float32 [768, 3072], P('shard')
- grad_down_weight: float32 [3072, 768], P('shard')
- grad_query_bias: float32 [768], P('shard')
- grad_value_bias: float32 [768], P('shard')
- grad_out_bias: float32 [768], P('shard')
- grad_up_bias: float32 [3072], P('shard')
- grad_down_bias: float32 [768], P('shard')
- grad_first_gain: float32 [768], P('shard')
- grad_first_shift: float32 [768], P('shard')
- grad_second_gain: float32 [768], P('shard')
- grad_second_shift: float32 [768], P('shard')
Inputs may be any that keep to these rules, and one draw needn't show every extreme that they name: `segment_ids`: in each row of one device's packed rows the ids never fall; every id from 0 to 5 covers 1 to 256 consecutive rows, and one covers exactly 256. `send_order`: each row is a permutation of 0 to 511. `pack_order`: each row is a permutation of 0 to 511.
All inputs are finite; a program needn't handle non-finite values.
Results may differ from a plain program's by a relative error of at most 0.02.
Values may be sent and summed in bfloat16 or wider, within the bound.
No kernel may reach another device: no remote copies, remote signals or barrier semaphores. Data moves between devices by JAX's collectives and lax.ppermute only.
A program may use at most 128 MiB of HBM per device.

v0:
```python
import jax
import jax.numpy as jnp
from jax import lax
from jax.sharding import PartitionSpec as P

HEADS = 12
HEAD_DIM = 64


epsilon = 1e-12
inv_root_two = 0.7071067811865476
inv_root_tau = 0.3989422804014327


def project(left_rows, weight):
    return jnp.dot(left_rows, weight, preferred_element_type=jnp.float32)


def project_back(left_rows, weight):
    return jnp.einsum("ti,ji->tj", left_rows, weight, preferred_element_type=jnp.float32)


def outer_sum(left_rows, right_rows):
    return jnp.einsum("ti,tj->ij", left_rows, right_rows, preferred_element_type=jnp.float32)


def normalize(summed):
    center = summed - jnp.mean(summed, -1, keepdims=True)
    spread = lax.rsqrt(jnp.mean(center * center, -1, keepdims=True) + epsilon)
    return (center * spread, spread)


def norm_back(gradient, normed, spread):
    return spread * (
        gradient
        - jnp.mean(gradient, -1, keepdims=True)
        - normed * jnp.mean(gradient * normed, -1, keepdims=True)
    )


def inverse(order_rows):
    return (
        jnp.zeros_like(order_rows)
        .at[order_rows]
        .set(jnp.arange(order_rows.shape[0], dtype=jnp.int32))
    )


def masked_scores(query_part, key_rows, seg_part, segments, scaling):
    logits = (
        jnp.einsum("qhd,khd->hqk", query_part, key_rows, preferred_element_type=jnp.float32)
        * scaling
    )
    same_segment = seg_part[:, None] == segments[None, :]
    return jnp.where(same_segment[None], logits, -1e30)


def attend(queries, key_rows, value_rows, segments, block_rows, scaling):
    blocks = queries.shape[0] // block_rows

    def one_block(carried, block_index):
        logits = masked_scores(queries, key_rows, segments, segments, scaling)
        row_max = jnp.max(logits, -1, keepdims=True)
        exponent = jnp.exp(logits - row_max)
        row_total = jnp.sum(exponent, -1, keepdims=True)
        softmax_low = (exponent / row_total).astype(jnp.bfloat16)
        mixture = jnp.einsum(
            "hqk,khd->qhd", softmax_low, value_rows, preferred_element_type=jnp.float32
        )
        return (carried, (mixture.astype(jnp.bfloat16), (row_max + jnp.log(row_total))[..., 0]))

    _, (mixtures, log_sums) = lax.scan(one_block, None, jnp.arange(blocks))
    return (mixtures.reshape(queries.shape), log_sums)


def attend_back(queries, key_rows, value_rows, segments, log_sums, grad_mixed, block_rows, scaling):

    def one_block(carried, block_item):
        grad_keys, grad_values = carried
        block_index, log_part = block_item
        logits = masked_scores(queries, key_rows, segments, segments, scaling)
        softmax_rows = jnp.exp(logits - log_part[..., None])
        grad_soft = jnp.einsum(
            "qhd,khd->hqk", grad_mixed, value_rows, preferred_element_type=jnp.float32
        )
        row_inner = jnp.sum(softmax_rows * grad_soft, -1, keepdims=True)
        grad_logits = (softmax_rows * (grad_soft - row_inner)).astype(jnp.bfloat16)
        grad_query_part = (
            jnp.einsum("hqk,khd->qhd", grad_logits, key_rows, preferred_element_type=jnp.float32)
            * scaling
        )
        grad_keys = (
            grad_keys
            + jnp.einsum("hqk,qhd->khd", grad_logits, queries, preferred_element_type=jnp.float32)
            * scaling
        )
        grad_values = grad_values + jnp.einsum(
            "hqk,qhd->khd",
            softmax_rows.astype(jnp.bfloat16),
            grad_mixed,
            preferred_element_type=jnp.float32,
        )
        return ((grad_keys, grad_values), grad_query_part)

    blocks = queries.shape[0] // block_rows
    zeros_heads = jnp.zeros(queries.shape, jnp.float32)
    (grad_keys, grad_values), grad_queries = lax.scan(
        one_block, (zeros_heads, zeros_heads), (jnp.arange(blocks), log_sums)
    )
    return (grad_queries.reshape(queries.shape), grad_keys, grad_values)


def shards(
    tokens,
    cotangent,
    segment_ids,
    send_order,
    pack_order,
    query_weight,
    key_weight,
    value_weight,
    out_weight,
    up_weight,
    down_weight,
    query_bias,
    value_bias,
    out_bias,
    up_bias,
    down_bias,
    first_gain,
    first_shift,
    second_gain,
    second_shift,
):
    row_count = tokens.shape[0]
    send_rows = send_order[0]
    pack_rows = pack_order[0]
    segments = segment_ids[0]
    arrived = (
        lax.all_to_all(
            tokens[send_rows], ("rep", "shard"), split_axis=0, concat_axis=0, tiled=True
        ),
        lax.all_to_all(
            cotangent[send_rows], ("rep", "shard"), split_axis=0, concat_axis=0, tiled=True
        ),
    )
    inputs = arrived[0][pack_rows]
    grad_result = arrived[1][pack_rows].astype(jnp.float32)
    weights = (
        lax.all_gather(query_weight, "shard", axis=0, tiled=True),
        lax.all_gather(key_weight, "shard", axis=0, tiled=True),
        lax.all_gather(value_weight, "shard", axis=0, tiled=True),
        lax.all_gather(out_weight, "shard", axis=0, tiled=True),
        lax.all_gather(up_weight, "shard", axis=0, tiled=True),
        lax.all_gather(down_weight, "shard", axis=0, tiled=True),
        lax.all_gather(query_bias, "shard", axis=0, tiled=True),
        lax.all_gather(value_bias, "shard", axis=0, tiled=True),
        lax.all_gather(out_bias, "shard", axis=0, tiled=True),
        lax.all_gather(up_bias, "shard", axis=0, tiled=True),
        lax.all_gather(down_bias, "shard", axis=0, tiled=True),
        lax.all_gather(first_gain, "shard", axis=0, tiled=True),
        lax.all_gather(first_shift, "shard", axis=0, tiled=True),
        lax.all_gather(second_gain, "shard", axis=0, tiled=True),
        lax.all_gather(second_shift, "shard", axis=0, tiled=True),
    )
    (
        query_mat,
        key_mat,
        value_mat,
        out_mat,
        up_mat,
        down_mat,
        query_add,
        value_add,
        out_add,
        up_add,
        down_add,
        gain_one,
        shift_one,
        gain_two,
        shift_two,
    ) = weights
    scaling = HEAD_DIM ** (-0.5)
    block_rows = min(512, row_count)
    head_shape = (row_count, HEADS, HEAD_DIM)
    queries = (
        (project(inputs, query_mat) + query_add.astype(jnp.float32))
        .astype(jnp.bfloat16)
        .reshape(head_shape)
    )
    key_rows = project(inputs, key_mat).astype(jnp.bfloat16).reshape(head_shape)
    value_rows = (
        (project(inputs, value_mat) + value_add.astype(jnp.float32))
        .astype(jnp.bfloat16)
        .reshape(head_shape)
    )
    attended, log_sums = attend(queries, key_rows, value_rows, segments, block_rows, scaling)
    attended = attended.reshape(row_count, -1)
    first_sum = inputs.astype(jnp.float32) + (
        project(attended, out_mat) + out_add.astype(jnp.float32)
    )
    first_normed, first_spread = normalize(first_sum)
    normed_one = (
        first_normed * gain_one.astype(jnp.float32) + shift_one.astype(jnp.float32)
    ).astype(jnp.bfloat16)
    pre_act = project(normed_one, up_mat) + up_add.astype(jnp.float32)
    activated = jax.nn.gelu(pre_act, approximate=False).astype(jnp.bfloat16)
    second_sum = normed_one.astype(jnp.float32) + (
        project(activated, down_mat) + down_add.astype(jnp.float32)
    )
    second_normed, second_spread = normalize(second_sum)
    layer_rows = (
        second_normed * gain_two.astype(jnp.float32) + shift_two.astype(jnp.float32)
    ).astype(jnp.bfloat16)
    later_weights = (
        lax.all_gather(query_weight, "shard", axis=0, tiled=True),
        lax.all_gather(key_weight, "shard", axis=0, tiled=True),
        lax.all_gather(value_weight, "shard", axis=0, tiled=True),
        lax.all_gather(out_weight, "shard", axis=0, tiled=True),
        lax.all_gather(up_weight, "shard", axis=0, tiled=True),
        lax.all_gather(down_weight, "shard", axis=0, tiled=True),
        lax.all_gather(query_bias, "shard", axis=0, tiled=True),
        lax.all_gather(value_bias, "shard", axis=0, tiled=True),
        lax.all_gather(out_bias, "shard", axis=0, tiled=True),
        lax.all_gather(up_bias, "shard", axis=0, tiled=True),
        lax.all_gather(down_bias, "shard", axis=0, tiled=True),
        lax.all_gather(first_gain, "shard", axis=0, tiled=True),
        lax.all_gather(first_shift, "shard", axis=0, tiled=True),
        lax.all_gather(second_gain, "shard", axis=0, tiled=True),
        lax.all_gather(second_shift, "shard", axis=0, tiled=True),
    )
    (
        query_mat,
        key_mat,
        value_mat,
        out_mat,
        up_mat,
        down_mat,
        query_add,
        value_add,
        out_add,
        up_add,
        down_add,
        gain_one,
        shift_one,
        gain_two,
        shift_two,
    ) = later_weights
    grad_gain_two = jnp.sum(grad_result * second_normed, 0)
    grad_shift_two = jnp.sum(grad_result, 0)
    grad_second = norm_back(
        grad_result * gain_two.astype(jnp.float32), second_normed, second_spread
    )
    grad_ffn = grad_second.astype(jnp.bfloat16)
    grad_down = outer_sum(activated, grad_ffn)
    grad_down_add = jnp.sum(grad_ffn.astype(jnp.float32), 0)
    gelu_slope = (
        0.5 * (1.0 + lax.erf(pre_act * inv_root_two))
        + pre_act * jnp.exp(-0.5 * pre_act * pre_act) * inv_root_tau
    )
    grad_pre = (project_back(grad_ffn, down_mat) * gelu_slope).astype(jnp.bfloat16)
    grad_up = outer_sum(normed_one, grad_pre)
    grad_up_add = jnp.sum(grad_pre.astype(jnp.float32), 0)
    grad_normed = grad_second + project_back(grad_pre, up_mat)
    grad_gain_one = jnp.sum(grad_normed * first_normed, 0)
    grad_shift_one = jnp.sum(grad_normed, 0)
    grad_first = norm_back(grad_normed * gain_one.astype(jnp.float32), first_normed, first_spread)
    grad_branch = grad_first.astype(jnp.bfloat16)
    grad_out = outer_sum(attended, grad_branch)
    grad_out_add = jnp.sum(grad_branch.astype(jnp.float32), 0)
    grad_attended = project_back(grad_branch, out_mat).astype(jnp.bfloat16).reshape(head_shape)
    grad_query_heads, grad_key_heads, grad_value_heads = attend_back(
        queries, key_rows, value_rows, segments, log_sums, grad_attended, block_rows, scaling
    )
    grad_queries = grad_query_heads.reshape(row_count, -1).astype(jnp.bfloat16)
    grad_keys = grad_key_heads.reshape(row_count, -1).astype(jnp.bfloat16)
    grad_values = grad_value_heads.reshape(row_count, -1).astype(jnp.bfloat16)
    grad_query = outer_sum(inputs, grad_queries)
    grad_key = outer_sum(inputs, grad_keys)
    grad_value = outer_sum(inputs, grad_values)
    grad_query_add = jnp.sum(grad_queries.astype(jnp.float32), 0)
    grad_value_add = jnp.sum(grad_values.astype(jnp.float32), 0)
    grad_inputs = (
        grad_first
        + project_back(grad_queries, query_mat)
        + project_back(grad_keys, key_mat)
        + project_back(grad_values, value_mat)
    )
    inverse_pack = inverse(pack_rows)
    inverse_send = inverse(send_rows)
    returned = (
        lax.all_to_all(
            layer_rows[inverse_pack], ("rep", "shard"), split_axis=0, concat_axis=0, tiled=True
        ),
        lax.all_to_all(
            grad_inputs.astype(jnp.bfloat16)[inverse_pack],
            ("rep", "shard"),
            split_axis=0,
            concat_axis=0,
            tiled=True,
        ),
    )
    layer_back = returned[0][inverse_send]
    grad_back = returned[1][inverse_send]
    (
        share_query,
        share_key,
        share_value,
        share_out,
        share_up,
        share_down,
        share_query_add,
        share_value_add,
        share_out_add,
        share_up_add,
        share_down_add,
        share_gain_one,
        share_shift_one,
        share_gain_two,
        share_shift_two,
    ) = (
        lax.psum_scatter(
            grad_query.astype(jnp.bfloat16), "shard", scatter_dimension=0, tiled=True
        ).astype(jnp.float32),
        lax.psum_scatter(
            grad_key.astype(jnp.bfloat16), "shard", scatter_dimension=0, tiled=True
        ).astype(jnp.float32),
        lax.psum_scatter(
            grad_value.astype(jnp.bfloat16), "shard", scatter_dimension=0, tiled=True
        ).astype(jnp.float32),
        lax.psum_scatter(
            grad_out.astype(jnp.bfloat16), "shard", scatter_dimension=0, tiled=True
        ).astype(jnp.float32),
        lax.psum_scatter(
            grad_up.astype(jnp.bfloat16), "shard", scatter_dimension=0, tiled=True
        ).astype(jnp.float32),
        lax.psum_scatter(
            grad_down.astype(jnp.bfloat16), "shard", scatter_dimension=0, tiled=True
        ).astype(jnp.float32),
        lax.psum_scatter(
            grad_query_add.astype(jnp.bfloat16), "shard", scatter_dimension=0, tiled=True
        ).astype(jnp.float32),
        lax.psum_scatter(
            grad_value_add.astype(jnp.bfloat16), "shard", scatter_dimension=0, tiled=True
        ).astype(jnp.float32),
        lax.psum_scatter(
            grad_out_add.astype(jnp.bfloat16), "shard", scatter_dimension=0, tiled=True
        ).astype(jnp.float32),
        lax.psum_scatter(
            grad_up_add.astype(jnp.bfloat16), "shard", scatter_dimension=0, tiled=True
        ).astype(jnp.float32),
        lax.psum_scatter(
            grad_down_add.astype(jnp.bfloat16), "shard", scatter_dimension=0, tiled=True
        ).astype(jnp.float32),
        lax.psum_scatter(
            grad_gain_one.astype(jnp.bfloat16), "shard", scatter_dimension=0, tiled=True
        ).astype(jnp.float32),
        lax.psum_scatter(
            grad_shift_one.astype(jnp.bfloat16), "shard", scatter_dimension=0, tiled=True
        ).astype(jnp.float32),
        lax.psum_scatter(
            grad_gain_two.astype(jnp.bfloat16), "shard", scatter_dimension=0, tiled=True
        ).astype(jnp.float32),
        lax.psum_scatter(
            grad_shift_two.astype(jnp.bfloat16), "shard", scatter_dimension=0, tiled=True
        ).astype(jnp.float32),
    )
    owned_grads = (
        lax.psum(share_query.astype(jnp.bfloat16), "rep").astype(jnp.float32),
        lax.psum(share_key.astype(jnp.bfloat16), "rep").astype(jnp.float32),
        lax.psum(share_value.astype(jnp.bfloat16), "rep").astype(jnp.float32),
        lax.psum(share_out.astype(jnp.bfloat16), "rep").astype(jnp.float32),
        lax.psum(share_up.astype(jnp.bfloat16), "rep").astype(jnp.float32),
        lax.psum(share_down.astype(jnp.bfloat16), "rep").astype(jnp.float32),
        lax.psum(share_query_add.astype(jnp.bfloat16), "rep").astype(jnp.float32),
        lax.psum(share_value_add.astype(jnp.bfloat16), "rep").astype(jnp.float32),
        lax.psum(share_out_add.astype(jnp.bfloat16), "rep").astype(jnp.float32),
        lax.psum(share_up_add.astype(jnp.bfloat16), "rep").astype(jnp.float32),
        lax.psum(share_down_add.astype(jnp.bfloat16), "rep").astype(jnp.float32),
        lax.psum(share_gain_one.astype(jnp.bfloat16), "rep").astype(jnp.float32),
        lax.psum(share_shift_one.astype(jnp.bfloat16), "rep").astype(jnp.float32),
        lax.psum(share_gain_two.astype(jnp.bfloat16), "rep").astype(jnp.float32),
        lax.psum(share_shift_two.astype(jnp.bfloat16), "rep").astype(jnp.float32),
    )
    return (layer_back, grad_back, *owned_grads)


def solution(mesh):
    return jax.shard_map(
        shards,
        mesh=mesh,
        in_specs=(
            P(("rep", "shard"), None),
            P(("rep", "shard"), None),
            P(("rep", "shard"), None),
            P(("rep", "shard"), None),
            P(("rep", "shard"), None),
            P("shard", None),
            P("shard", None),
            P("shard", None),
            P("shard", None),
            P("shard", None),
            P("shard", None),
            P("shard"),
            P("shard"),
            P("shard"),
            P("shard"),
            P("shard"),
            P("shard"),
            P("shard"),
            P("shard"),
            P("shard"),
        ),
        out_specs=(
            P(("rep", "shard"), None),
            P(("rep", "shard"), None),
            P("shard", None),
            P("shard", None),
            P("shard", None),
            P("shard", None),
            P("shard", None),
            P("shard", None),
            P("shard"),
            P("shard"),
            P("shard"),
            P("shard"),
            P("shard"),
            P("shard"),
            P("shard"),
            P("shard"),
            P("shard"),
        ),
        check_vma=False,
    )
```

profile of v0, /device:TPU:0, one launch (start us, length us, event | category | flops | bytes accessed | tf_op | source)
XLA Modules:
  0.0 644.1 jit_solution(17305959502636402990)
XLA Ops:
  14.6 7.3 %all-to-all-start.2 = ((bf16[32,16,768]{2,1,0:T(8,128)(2,1)}), bf16[32,16,768]{2,1,0:T(8,128)(2,1)S(1)}, u32[]{:S(2)}, u32[]{:S(2)}) async-start(bf16[32,16,768]{2,1,0:T(8,128)(2,1)} %bitcast.16), calls=%async_computation.2 | async-start | bytes 1572864 | tf_op jit(solution)/shard_map/all_to_all | solution.py:143
  24.8 18.5 %all-to-all-done.2 = bf16[32,16,768]{2,1,0:T(8,128)(2,1)S(1)} async-done(((bf16[32,16,768]{2,1,0:T(8,128)(2,1)}), bf16[32,16,768]{2,1,0:T(8,128)(2,1)S(1)}, u32[]{:S(2)}, u32[]{:S(2)}) %all-to-all-start.2) | async-done | bytes 786464 | tf_op jit(solution)/shard_map/all_to_all | solution.py:143
  49.7 16.6 %all-reduce.20 = (bf16[768]{0:T(1024)(128)(2,1)S(1)}, bf16[768]{0:T(1024)(128)(2,1)S(1)}, bf16[768]{0:T(1024)(128)(2,1)S(1)}, bf16[768]{0:T(1024)(128)(2,1)S(1)}...) all-reduce(bf16[768]{0:T(1024)(128)(2,1)S(1)} %dynamic-update-slice, ...), channel_id=1, replica_groups=mesh['rep'=8,'shard'=4] {'shard'}, use_global_device_ids=true, to_apply=%add | all-reduce | flops 5376 | bytes 21504
  66.4 7.3 %all-gather = bf16[4,1,768]{2,1,0:T(2,128)(2,1)S(1)} all-gather(bf16[1,1,768]{2,1,0:T(2,128)(2,1)S(1)} %reshape.326), channel_id=1, replica_groups=mesh['rep'=8,'shard'=4] {'shard'}, dimensions={0}, use_global_device_ids=true | all-gather | bytes 7680 | tf_op jit(solution)/shard_map/all_gather | solution.py:159
  74.0 2.9 gather_fusion.5
  83.9 23.6 %all-gather.12.cloned.1.call-done = bf16[768,768]{1,0:T(8,128)(2,1)} async-done(((bf16[192,768]{1,0:T(8,128)(2,1)}), bf16[768,768]{1,0:T(8,128)(2,1)}) %all-gather.12.cloned.1.call-update) | async-done | bytes 1179664 | tf_op jit(solution)/shard_map/all_gather | solution.py:151
  116.5 4.4 fusion.33
  120.8 16.2 %all-gather.14.cloned.1.call-done = bf16[768,768]{1,0:T(8,128)(2,1)} async-done(((bf16[192,768]{1,0:T(8,128)(2,1)}), bf16[768,768]{1,0:T(8,128)(2,1)}) %all-gather.14.cloned.1.call-update) | async-done | bytes 1179664 | tf_op jit(solution)/shard_map/all_gather | solution.py:153
  140.0 55.8 %all-gather.16.cloned.1.call-done = bf16[768,3072]{1,0:T(8,128)(2,1)} async-done(((bf16[192,3072]{1,0:T(8,128)(2,1)}), bf16[768,3072]{1,0:T(8,128)(2,1)}) %all-gather.16.cloned.1.call-update) | async-done | bytes 4718608 | tf_op jit(solution)/shard_map/all_gather | solution.py:154
  195.8 19.3 %fusion.4 = (bf16[512,3072]{1,0:T(8,128)(2,1)}, f32[512,3072]{1,0:T(8,128)}) fusion(f32[3072]{0:T(1024)S(1)} %bitcast.96, bf16[768,3072]{1,0:T(8,128)(2,1)} %all-gather.16.cloned.1.call-done, f32[512,768]{1,0:T(8,128)S(1)} %get-tuple-element.117, f32[768]{0:T(1024)S(1)} %convert_element_type.245, f32[768]{0:T(1024)S(1)} %convert_element_type.244, ...), kind=kOutput, calls=%fused_computation.22 | convolution fusion | flops 2521694208 | bytes 15751168 | tf_op jit(solution)/shard_map/dot_general | solution.py:16
  215.1 39.5 %all-gather.18.cloned.1.call-done = bf16[3072,768]{1,0:T(8,128)(2,1)} async-done(((bf16[768,768]{1,0:T(8,128)(2,1)}), bf16[3072,768]{1,0:T(8,128)(2,1)}) %all-gather.18.cloned.1.call-update) | async-done | bytes 4718608 | tf_op jit(solution)/shard_map/all_gather | solution.py:155
  254.6 6.6 %fusion.49 = (f32[512]{0:T(512)S(1)}, f32[512,768]{1,0:T(8,128)S(1)}) fusion(f32[768]{0:T(1024)S(1)} %convert_element_type.250, bf16[512,3072]{1,0:T(8,128)(2,1)} %get-tuple-element.118, bf16[3072,768]{1,0:T(8,128)(2,1)} %all-gather.18.cloned.1.call-done, f32[768]{0:T(1024)S(1)} %convert_element_type.245, f32[768]{0:T(1024)S(1)} %convert_element_type.244, ...), kind=kOutput, calls=%fused_computation.119 | convolution fusion | flops 2419457536 | bytes 11025408 | tf_op jit(solution)/shard_map/dot_general | solution.py:16
  263.9 5.7 fusion.52
  269.6 3.6 multiply_reduce_fusion.1
  276.8 3.4 convolution_convert_fusion.6
  282.6 8.2 %fusion.51 = (bf16[12,64]{1,0:T(8,128)(2,1)S(1)}, bf16[12,64,512]{2,1,0:T(8,128)(2,1)S(1)}) fusion(bf16[512,12,64]{0,2,1:T(8,128)(2,1)} %bitcast.86, f32[12,512]{1,0:T(8,128)S(1)} %log_add_fusion, f32[12,512,512]{1,2,0:T(8,128)} %copy-done.2, pred[512,512]{0,1:T(8,128)(4,1)S(1)} %broadcast_compare_fusion), kind=kOutput, calls=%fused_computation.121 | convolution fusion | flops 416021760 | bytes 14444032 | tf_op jit(solution)/shard_map/while/body/eval_jaxpr/hqk,qhd->khd/dot_general | solution.py:97
  293.9 9.3 %multiply_reduce_fusion = (f32[12,512]{1,0:T(8,128)S(1)}, f32[12,512,512]{1,2,0:T(8,128)S(1)}) fusion(f32[12,512]{1,0:T(8,128)S(1)} %log_add_fusion, f32[12,512,512]{1,2,0:T(8,128)} %copy-done.2, pred[512,512]{0,1:T(8,128)(4,1)S(1)} %broadcast_compare_fusion, bf16[512,12,64]{0,2,1:T(8,128)(2,1)} %bitcast.87, bf16[512,12,64]{0,2,1:T(8,128)(2,1)} %bitcast.85), kind=kOutput, calls=%fused_computation.11 | convolution fusion | flops 418375680 | bytes 27049984 | tf_op jit(solution)/shard_map/while/body/eval_jaxpr/qhd,khd->hqk/dot_general | solution.py:83
  303.3 7.0 %multiply_convert_fusion = bf16[12,512,512]{1,2,0:T(8,128)(2,1)S(1)} fusion(f32[12,512,512]{1,2,0:T(8,128)S(1)} %get-tuple-element.124, f32[12,512]{1,0:T(8,128)S(1)} %get-tuple-element.123, f32[12,512]{1,0:T(8,128)S(1)} %log_add_fusion, f32[12,512,512]{1,2,0:T(8,128)} %copy-done.2, pred[512,512]{0,1:T(8,128)(4,1)S(1)} %broadcast_compare_fusion), kind=kLoop, calls=%fused_computation.10 | loop fusion | flops 18874368 | bytes 31768576 | tf_op jit(solution)/shard_map/while/body/eval_jaxpr/convert_element_type | solution.py:87
  315.8 4.8 multiply_convert_fusion.1
  323.5 7.4 %convolution_convert_fusion.1 = bf16[768,3072]{1,0:T(8,128)(2,1)} fusion(bf16[512,3072]{1,0:T(8,128)(2,1)} %copy-done.41, f32[512,768]{1,0:T(8,128)} %copy-done.8, f32[768]{0:T(1024)S(1)} %convert_element_type.245, f32[768]{0:T(1024)S(1)} %convert_element_type.244, f32[512]{0:T(512)S(1)} %add_rsqrt_fusion.1, f32[512]{0:T(512)S(1)} %broadcast_multiply_fusion.5), kind=kOutput, calls=%fused_computation.48 | convolution fusion | flops 2420244480 | bytes 9447424 | tf_op jit(solution)/shard_map/ti,tj->ij/dot_general | solution.py:24
  331.2 7.2 %convolution_convert_fusion = bf16[3072,768]{1,0:T(8,128)(2,1)} fusion(bf16[512,3072]{1,0:T(8,128)(2,1)} %get-tuple-element.118, f32[512,768]{1,0:T(8,128)} %copy-done.13), kind=kOutput, calls=%fused_computation.47 | convolution fusion | flops 2418671616 | bytes 9437184 | tf_op jit(solution)/shard_map/ti,tj->ij/dot_general | solution.py:24
  341.9 15.7 %all-reduce.19 = (bf16[768]{0:T(1024)(128)(2,1)S(1)}, bf16[768]{0:T(1024)(128)(2,1)S(1)}, bf16[768]{0:T(1024)(128)(2,1)S(1)}, bf16[768]{0:T(1024)(128)(2,1)S(1)}...) all-reduce(bf16[768]{0:T(1024)(128)(2,1)S(1)} %dynamic-update-slice, ...), channel_id=1, replica_groups=mesh['rep'=8,'shard'=4] {'shard'}, use_global_device_ids=true, to_apply=%add.7 | all-reduce | flops 9984 | bytes 39936
  360.6 4.5 all-to-all-start.1
  365.2 3.2 fusion.53
  368.5 3.4 fusion.54
  371.8 29.2 %reduce-scatter.9.cloned.1.call-done = bf16[192,768]{1,0:T(8,128)(2,1)} async-done(((bf16[768,768]{1,0:T(8,128)(2,1)}), bf16[192,768]{1,0:T(8,128)(2,1)}) %reduce-scatter.9.cloned.1.call-update) | async-done | bytes 294928 | tf_op jit(solution)/shard_map/reduce_scatter | solution.py:325
  401.1 60.1 %reduce-scatter.15.cloned.1.call-done = bf16[192,3072]{1,0:T(8,128)(2,1)} async-done(((bf16[768,3072]{1,0:T(8,128)(2,1)}), bf16[192,3072]{1,0:T(8,128)(2,1)}) %reduce-scatter.15.cloned.1.call-update) | async-done | bytes 1179664 | tf_op jit(solution)/shard_map/reduce_scatter | solution.py:334
  461.2 60.0 %reduce-scatter.17.cloned.1.call-done = bf16[768,768]{1,0:T(8,128)(2,1)} async-done(((bf16[3072,768]{1,0:T(8,128)(2,1)}), bf16[768,768]{1,0:T(8,128)(2,1)}) %reduce-scatter.17.cloned.1.call-update) | async-done | bytes 1179664 | tf_op jit(solution)/shard_map/reduce_scatter | solution.py:337
  521.2 3.3 add_convert_fusion
  527.2 4.6 all-to-all-start.3
  536.4 34.1 %all-reduce.17 = (bf16[192]{0:T(256)(128)(2,1)S(1)}, bf16[192]{0:T(256)(128)(2,1)S(1)}, bf16[192]{0:T(256)(128)(2,1)S(1)}, bf16[768]{0:T(1024)(128)(2,1)S(1)}, b...) all-reduce(bf16[192]{0:T(256)(128)(2,1)S(1)} %dynamic-slice.9, ...), channel_id=1, replica_groups=mesh['rep'=8,'shard'=4] {'rep'}, use_global_device_ids=true, to_apply=%region_27.28 | all-reduce | flops 2304 | bytes 9216 | tf_op jit(solution)/shard_map/psum | solution.py:375
  581.0 45.6 %all-reduce.23.cloned.1.call-done = (bf16[192,768]{1,0:T(8,128)(2,1)}, bf16[192,768]{1,0:T(8,128)(2,1)}, bf16[192,768]{1,0:T(8,128)(2,1)}, bf16[192,768]{1,0:T(8...) async-done(((bf16[192,768]{1,0:T(8,128)(2,1)}, bf16[192,768]{1,0:T(8,128)(2,1)}, bf16[192,768]{1,0:T(8,128)(2,1)}, bf16[192,768]{1,0:T(8,128)(2,1)}, ...) | async-done | bytes 3538960 | tf_op jit(solution)/shard_map/psum | solution.py:369
  (228 shorter events, 88.6 us)
Async XLA Ops:
  7.2 71.7 %all-gather.10.cloned.1.call-start = ((), (), s32[]{:S(2)}) async-start(), calls=%async_computation.11 | async-start | bytes 1474560 | tf_op jit(solution)/shard_map/all_gather | solution.py:150
  7.9 73.6 %all-gather.8.cloned.1.call-start = ((), (), s32[]{:S(2)}) async-start(), calls=%async_computation.10 | async-start | bytes 1474560 | tf_op jit(solution)/shard_map/all_gather | solution.py:152
  8.7 98.9 %all-gather.12.cloned.1.call-start = ((), (), s32[]{:S(2)}) async-start(), calls=%async_computation.12 | async-start | bytes 1474560 | tf_op jit(solution)/shard_map/all_gather | solution.py:151
  9.4 127.6 %all-gather.14.cloned.1.call-start = ((), (), s32[]{:S(2)}) async-start(), calls=%async_computation.13 | async-start | bytes 1474560 | tf_op jit(solution)/shard_map/all_gather | solution.py:153
  10.0 185.8 %all-gather.16.cloned.1.call-start = ((), (), s32[]{:S(2)}) async-start(), calls=%async_computation.14 | async-start | bytes 5898240 | tf_op jit(solution)/shard_map/all_gather | solution.py:154
  14.6 28.7 %all-to-all-start.2 = ((bf16[32,16,768]{2,1,0:T(8,128)(2,1)}), bf16[32,16,768]{2,1,0:T(8,128)(2,1)S(1)}, u32[]{:S(2)}, u32[]{:S(2)}) async-start(bf16[32,16,768]{2,1,0:T(8,128)(2,1)} %bitcast.16), calls=%async_computation.2 | async-start | bytes 1572864 | tf_op jit(solution)/shard_map/all_to_all | solution.py:143
  21.9 24.9 %copy-start.29 = (u32[32]{0:T(128)S(1)}, u32[32]{0:T(128)}, u32[]{:S(2)}) copy-start(u32[32]{0:T(128)} %constant.132) | copy-start | bytes 388
  21.9 26.1 %copy-start.33 = (bf16[192]{0:T(256)(128)(2,1)S(1)}, bf16[192]{0:T(256)(128)(2,1)}, u32[]{:S(2)}) copy-start(bf16[192]{0:T(256)(128)(2,1)} %param.38) | copy-start | bytes 1156
  21.9 26.4 %copy-start.34 = (bf16[192]{0:T(256)(128)(2,1)S(1)}, bf16[192]{0:T(256)(128)(2,1)}, u32[]{:S(2)}) copy-start(bf16[192]{0:T(256)(128)(2,1)} %param.35) | copy-start | bytes 1156
  21.9 26.6 %copy-start.35 = (bf16[192]{0:T(256)(128)(2,1)S(1)}, bf16[192]{0:T(256)(128)(2,1)}, u32[]{:S(2)}) copy-start(bf16[192]{0:T(256)(128)(2,1)} %param.36) | copy-start | bytes 1156
  22.0 26.8 %copy-start.36 = (bf16[192]{0:T(256)(128)(2,1)S(1)}, bf16[192]{0:T(256)(128)(2,1)}, u32[]{:S(2)}) copy-start(bf16[192]{0:T(256)(128)(2,1)} %param.37) | copy-start | bytes 1156
  22.0 27.0 %copy-start.37 = (bf16[192]{0:T(256)(128)(2,1)S(1)}, bf16[192]{0:T(256)(128)(2,1)}, u32[]{:S(2)}) copy-start(bf16[192]{0:T(256)(128)(2,1)} %param.33) | copy-start | bytes 1156
  22.0 27.3 %copy-start.38 = (bf16[192]{0:T(256)(128)(2,1)S(1)}, bf16[192]{0:T(256)(128)(2,1)}, u32[]{:S(2)}) copy-start(bf16[192]{0:T(256)(128)(2,1)} %param.31) | copy-start | bytes 1156
  22.0 27.5 %copy-start.39 = (bf16[192]{0:T(256)(128)(2,1)S(1)}, bf16[192]{0:T(256)(128)(2,1)}, u32[]{:S(2)}) copy-start(bf16[192]{0:T(256)(128)(2,1)} %param.32) | copy-start | bytes 1156
  22.0 44.3 %copy-start.30 = (bf16[768]{0:T(1024)(128)(2,1)S(1)}, bf16[768]{0:T(1024)(128)(2,1)}, u32[]{:S(2)}) copy-start(bf16[768]{0:T(1024)(128)(2,1)} %param.34) | copy-start | bytes 4612
  22.0 51.7 %copy-start.31 = (s32[1,512]{1,0:T(1,128)S(1)}, s32[1,512]{1,0:T(1,128)}, u32[]{:S(2)}) copy-start(s32[1,512]{1,0:T(1,128)} %param.24) | copy-start | bytes 6148
  22.0 51.7 %copy-start.24 = (s32[1,512]{1,0:T(1,128)S(1)}, s32[1,512]{1,0:T(1,128)}, u32[]{:S(2)}) copy-start(s32[1,512]{1,0:T(1,128)} %param.22) | copy-start | bytes 6148
  43.3 33.6 %all-to-all-start = ((bf16[32,16,768]{2,1,0:T(8,128)(2,1)}), bf16[32,16,768]{2,1,0:T(8,128)(2,1)S(1)}, u32[]{:S(2)}, u32[]{:S(2)}) async-start(bf16[32,16,768]{2,1,0:T(8,128)(2,1)} %bitcast.2), calls=%async_computation | async-start | bytes 1572864 | tf_op jit(solution)/shard_map/all_to_all | solution.py:140
  46.1 208.4 %all-gather.18.cloned.1.call-start = ((), (), s32[]{:S(2)}) async-start(), calls=%async_computation.15 | async-start | bytes 5898240 | tf_op jit(solution)/shard_map/all_gather | solution.py:155
  46.7 325.1 %reduce-scatter.13.cloned.1.call-start = ((), (), s32[]{:S(2)}) async-start(), calls=%async_computation.19 | async-start | bytes 1474560 | tf_op jit(solution)/shard_map/reduce_scatter | solution.py:331
  78.9 28.6 %copy-start.18 = (bf16[512,768]{1,0:T(8,128)(2,1)}, bf16[512,768]{1,0:T(8,128)(2,1)S(1)}, u32[]{:S(2)}) copy-start(bf16[512,768]{1,0:T(8,128)(2,1)S(1)} %gather_fusion.1) | copy-start | bytes 2359300
  83.9 30.6 %copy-start.10 = (bf16[512,768]{0,1:T(8,128)(2,1)}, bf16[512,768]{0,1:T(8,128)(2,1)S(1)}, u32[]{:S(2)}) copy-start(bf16[512,768]{0,1:T(8,128)(2,1)S(1)} %copy.57) | copy-start | bytes 2359300
  139.7 75.4 %copy-start.8 = (f32[512,768]{1,0:T(8,128)}, f32[512,768]{1,0:T(8,128)S(1)}, u32[]{:S(2)}) copy-start(f32[512,768]{1,0:T(8,128)S(1)} %get-tuple-element.117) | copy-start | bytes 4718596
  276.7 95.1 %reduce-scatter.11.cloned.1.call-start = ((), (), s32[]{:S(2)}) async-start(), calls=%async_computation.18 | async-start | bytes 1474560 | tf_op jit(solution)/shard_map/reduce_scatter | solution.py:328
  293.7 78.1 %reduce-scatter.7.cloned.1.call-start = ((), (), s32[]{:S(2)}) async-start(), calls=%async_computation.16 | async-start | bytes 1474560 | tf_op jit(solution)/shard_map/reduce_scatter | solution.py:322
  315.7 85.3 %reduce-scatter.9.cloned.1.call-start = ((), (), s32[]{:S(2)}) async-start(), calls=%async_computation.17 | async-start | bytes 1474560 | tf_op jit(solution)/shard_map/reduce_scatter | solution.py:325
  323.4 137.8 %reduce-scatter.15.cloned.1.call-start = ((), (), s32[]{:S(2)}) async-start(), calls=%async_computation.20 | async-start | bytes 5898240 | tf_op jit(solution)/shard_map/reduce_scatter | solution.py:334
  330.9 190.3 %reduce-scatter.17.cloned.1.call-start = ((), (), s32[]{:S(2)}) async-start(), calls=%async_computation.21 | async-start | bytes 5898240 | tf_op jit(solution)/shard_map/reduce_scatter | solution.py:337
  360.6 166.6 %all-to-all-start.1 = ((bf16[32,16,768]{2,1,0:T(8,128)(2,1)}), bf16[32,16,768]{2,1,0:T(8,128)(2,1)S(1)}, u32[]{:S(2)}, u32[]{:S(2)}) async-start(bf16[32,16,768]{2,1,0:T(8,128)(2,1)} %bitcast.14), calls=%async_computation.1 | async-start | bytes 1572864 | tf_op jit(solution)/shard_map/all_to_all | solution.py:292
  365.2 261.4 %all-reduce.23.cloned.1.call-start = ((), (), s32[]{:S(2)}) async-start(), calls=%async_computation.22 | async-start | bytes 7077888 | tf_op jit(solution)/shard_map/psum | solution.py:369
  368.5 152.7 %copy-start.6 = (f32[512,768]{1,0:T(8,128)S(1)}, f32[512,768]{1,0:T(8,128)}, u32[]{:S(2)}) copy-start(f32[512,768]{1,0:T(8,128)} %copy-done.5) | copy-start | bytes 4718596
  527.2 51.1 %all-to-all-start.3 = ((bf16[32,16,768]{2,1,0:T(8,128)(2,1)}), bf16[32,16,768]{2,1,0:T(8,128)(2,1)S(1)}, u32[]{:S(2)}, u32[]{:S(2)}) async-start(bf16[32,16,768]{2,1,0:T(8,128)(2,1)} %bitcast.25), calls=%async_computation.3 | async-start | bytes 1572864 | tf_op jit(solution)/shard_map/all_to_all | solution.py:295
  (30 other events, 137.3 us)
Sparse Core Ops, SparseCore 0:
  9.9 37.5 all-gather.9
  49.3 28.5 all-gather.7
  79.8 27.7 all-gather.11
  109.2 27.7 all-gather.13
  138.7 57.0 all-gather.15
  197.5 57.0 all-gather.17
  276.9 28.5 reduce-scatter.12
  308.4 28.5 reduce-scatter.10
  339.9 28.7 reduce-scatter.6
  371.4 29.5 reduce-scatter.8
  404.1 57.0 reduce-scatter.14
  464.0 57.0 reduce-scatter.16
  524.0 102.5 all-reduce.22
where the time goes:
time: 649 us; the launch traced here: 644 us
  waiting for transfers between devices  352 us (54%)
  matrix products  110 us (17%)
  blocking collectives  73.7 us (11%)
  local copies, waits for them, and re-layouts  41.9 us (6%)
  other arithmetic  29.3 us (5%)
  starting transfers between devices  20.2 us (3%)
  between operations  16.8 us (3%)
    reduce_scatter x1, waiting for transfers between devices, shards(): lax.psum_scatter(grad_up.astype(jnp.bfloat16), 'shard', scatter_dimension...  60.1 us
    reduce_scatter x1, waiting for transfers between devices, shards(): lax.psum_scatter(grad_down.astype(jnp.bfloat16), 'shard', scatter_dimensi...  60 us
    all_gather x1, waiting for transfers between devices, shards(): lax.all_gather(up_weight, 'shard', axis=0, tiled=True)  55.8 us
    psum x1, waiting for transfers between devices, shards(): lax.psum(share_query.astype(jnp.bfloat16), 'rep').astype(jnp.float32)  45.6 us
    all_gather x1, waiting for transfers between devices, shards(): lax.all_gather(down_weight, 'shard', axis=0, tiled=True)  39.5 us
    dot_general x6, matrix products, project(): return jnp.dot(left_rows, weight, preferred_element_type=jnp.float32)  34.9 us
    psum x1, blocking collectives, shards(): lax.psum(share_query_add.astype(jnp.bfloat16), 'rep').astype(jnp.float32)  34.1 us
    unnamed x2, blocking collectives  32.4 us
  transfers between devices with their start and end apart: 17, of which 9 were waited for; matrix products, arithmetic and copies ran while one was open for 22% of the time, Pallas kernels for 0%

commit v1 on v0

v1 whole, which is shorter than its diff:
```python
import functools

import jax
import jax.numpy as jnp
from jax import lax
from jax.experimental import pallas as pl
from jax.experimental.pallas import tpu as pltpu
from jax.sharding import PartitionSpec as P

HEADS = 12
HEAD_DIM = 64
VEC_ROWS = 32

epsilon = 1e-12
inv_root_two = 0.7071067811865476
inv_root_tau = 0.3989422804014327
BF = jnp.bfloat16
F32 = jnp.float32
ANY = pl.BlockSpec(memory_space=pl.ANY)
SMEM = pl.BlockSpec(memory_space=pltpu.SMEM)


def project(left_rows, weight):
    return jnp.dot(left_rows, weight, preferred_element_type=F32)


def project_back(left_rows, weight):
    return jnp.einsum("ti,ji->tj", left_rows, weight, preferred_element_type=F32)


def outer_sum(left_rows, right_rows):
    return jnp.einsum("ti,tj->ij", left_rows, right_rows, preferred_element_type=F32)


def normalize(summed):
    center = summed - jnp.mean(summed, -1, keepdims=True)
    spread = lax.rsqrt(jnp.mean(center * center, -1, keepdims=True) + epsilon)
    return (center * spread, spread)


def norm_back(gradient, normed, spread):
    return spread * (
        gradient
        - jnp.mean(gradient, -1, keepdims=True)
        - normed * jnp.mean(gradient * normed, -1, keepdims=True)
    )


def inverse(order_rows):
    return (
        jnp.zeros_like(order_rows)
        .at[order_rows]
        .set(jnp.arange(order_rows.shape[0], dtype=jnp.int32))
    )


class Comm:
    def __init__(self, mesh):
        self.S = mesh.shape["shard"]
        self.R = mesh.shape["rep"]
        self.Z = self.R // 2
        self.groups = [[r for r in range(self.R) if r % 2 == c] for c in range(2)]

    def across(self, x, mask):
        return lax.ppermute(x, "shard", [(i, i ^ mask) for i in range(self.S)])

    def partner(self, x):
        return lax.ppermute(x, "rep", [(i, i ^ 1) for i in range(self.R)])

    def over_z(self, x):
        return lax.all_to_all(
            x, "rep", split_axis=0, concat_axis=0, tiled=True, axis_index_groups=self.groups
        )

    def gather(self, part):
        if self.S != 4:
            got = [(r, 0, self.across(part, r)) for r in range(1, self.S)]
        else:
            half = part.shape[0] // 2
            from_x = self.across(part, 1)
            from_y = self.across(part, 2)
            low = self.across(from_x[:half], 2)
            high = self.across(from_y[half:], 1)
            got = [(1, 0, from_x), (2, 0, from_y), (3, 0, low), (3, half, high)]
        return got + [(r, at, self.partner(piece)) for r, at, piece in got]

    def reduce_shard(self, parts, s):
        rel = [lax.dynamic_index_in_dim(parts, s ^ r, 0, keepdims=False) for r in range(self.S)]
        if self.S != 4:
            total = rel[0].astype(F32)
            for r in range(1, self.S):
                total = total + self.across(rel[r], r).astype(F32)
            return total.astype(BF)
        half = parts.shape[1] // 2

        def add(a, b):
            return (a.astype(F32) + b.astype(F32)).astype(BF)

        low = self.across(jnp.concatenate([rel[1][:half], rel[3][:half]]), 1)
        high = self.across(jnp.concatenate([rel[2][half:], rel[3][half:]]), 2)
        low2 = self.across(add(rel[2][:half], low[half:]), 2)
        high1 = self.across(add(rel[1][half:], high[half:]), 1)
        low0 = rel[0][:half].astype(F32) + low[:half].astype(F32) + low2.astype(F32)
        high0 = rel[0][half:].astype(F32) + high[:half].astype(F32) + high1.astype(F32)
        return jnp.concatenate([low0, high0]).astype(BF)

    def reduce(self, mine, theirs, s):
        summed = (mine.astype(F32) + self.partner(theirs).astype(F32)).astype(BF)
        own = self.reduce_shard(summed, s)
        h, n = own.shape
        spread = self.over_z(own.reshape(self.Z, h // self.Z, n))
        total = jnp.sum(spread.astype(F32), 0).astype(BF)
        again = self.over_z(jnp.broadcast_to(total[None], (self.Z,) + total.shape))
        half = again.reshape(h, n)
        return half, self.partner(half)


def assemble(where, owns, got, shard_rows, halves):
    count = len(owns)
    S = where[2]

    def body(pos, *refs):
        own_refs = refs[:count]
        piece_refs = refs[count : count + len(got)]
        outs = refs[count + len(got) : 2 * count + len(got)]
        sem = refs[-1]
        s = pos[0]
        c = pos[1]
        copies = []
        for w in range(count):
            copies.append((own_refs[w], outs[w].at[pl.ds(s * shard_rows[w], shard_rows[w])]))
        for i, (r, at, piece) in enumerate(got):
            core = c if i < len(got) // 2 else 1 - c
            base = 0
            for w in range(count):
                lo, hi = max(at, base), min(at + piece.shape[0], base + halves[w])
                if lo < hi:
                    row = (s ^ r) * shard_rows[w] + core * halves[w] + (lo - base)
                    row = pl.multiple_of(row, 8)
                    copies.append(
                        (piece_refs[i].at[pl.ds(lo - at, hi - lo)], outs[w].at[pl.ds(row, hi - lo)])
                    )
                base += halves[w]
        copies = [pltpu.make_async_copy(a, b, sem.at[i]) for i, (a, b) in enumerate(copies)]
        for copy in copies:
            copy.start()
        for copy in copies:
            copy.wait()

    total = count + sum(
        sum(
            1
            for w in range(count)
            if max(at, sum(halves[:w])) < min(at + piece.shape[0], sum(halves[: w + 1]))
        )
        for r, at, piece in got
    )
    return pl.pallas_call(
        body,
        out_shape=[
            jax.ShapeDtypeStruct((S * rows, own.shape[1]), BF) for rows, own in zip(shard_rows, owns)
        ],
        in_specs=[SMEM] + [ANY] * (count + len(got)),
        out_specs=[pl.BlockSpec(memory_space=pltpu.VMEM)] * count,
        scratch_shapes=[pltpu.SemaphoreType.DMA((total,))],
        name="assemble",
    )(jnp.stack([where[0], where[1]]), *owns, *[g[2] for g in got])


def masked_scores(query_part, key_rows, segments, scaling):
    logits = jnp.einsum("qhd,khd->hqk", query_part, key_rows, preferred_element_type=F32) * scaling
    same_segment = segments[:, None] == segments[None, :]
    return jnp.where(same_segment[None], logits, -1e30)


def attend(queries, key_rows, value_rows, segments, scaling):
    logits = masked_scores(queries, key_rows, segments, scaling)
    row_max = jnp.max(logits, -1, keepdims=True)
    exponent = jnp.exp(logits - row_max)
    row_total = jnp.sum(exponent, -1, keepdims=True)
    softmax_low = (exponent / row_total).astype(BF)
    mixture = jnp.einsum("hqk,khd->qhd", softmax_low, value_rows, preferred_element_type=F32)
    return mixture.astype(BF), (row_max + jnp.log(row_total))[..., 0]


def attend_back(queries, key_rows, value_rows, segments, log_sums, grad_mixed, scaling):
    logits = masked_scores(queries, key_rows, segments, scaling)
    softmax_rows = jnp.exp(logits - log_sums[..., None])
    grad_soft = jnp.einsum("qhd,khd->hqk", grad_mixed, value_rows, preferred_element_type=F32)
    row_inner = jnp.sum(softmax_rows * grad_soft, -1, keepdims=True)
    grad_logits = (softmax_rows * (grad_soft - row_inner)).astype(BF)
    grad_queries = (
        jnp.einsum("hqk,khd->qhd", grad_logits, key_rows, preferred_element_type=F32) * scaling
    )
    grad_keys = (
        jnp.einsum("hqk,qhd->khd", grad_logits, queries, preferred_element_type=F32) * scaling
    )
    grad_values = jnp.einsum(
        "hqk,qhd->khd", softmax_rows.astype(BF), grad_mixed, preferred_element_type=F32
    )
    return grad_queries, grad_keys, grad_values


def shards(
    comm,
    tokens,
    cotangent,
    segment_ids,
    send_order,
    pack_order,
    query_weight,
    key_weight,
    value_weight,
    out_weight,
    up_weight,
    down_weight,
    *vectors,
):
    S = comm.S
    s = lax.axis_index("shard")
    c = lax.axis_index("rep") % 2
    pos = (s, c, S)
    row_count, width = tokens.shape
    send_rows = send_order[0]
    pack_rows = pack_order[0]
    segments = segment_ids[0]

    def exchange(rows):
        return lax.all_to_all(rows, ("rep", "shard"), split_axis=0, concat_axis=0, tiled=True)

    def my_half(weight):
        half = weight.shape[0] // 2
        return lax.dynamic_slice_in_dim(weight, c * half, half, 0)

    sizes = [v.shape[0] for v in vectors]
    packed = jnp.concatenate(vectors)
    packed = jnp.pad(packed, (0, VEC_ROWS * width - packed.shape[0])).reshape(VEC_ROWS, width)
    squares = (query_weight, key_weight, value_weight, out_weight)
    square_part = jnp.concatenate([my_half(w) for w in squares] + [packed])
    got_square = comm.gather(square_part)
    arrived = exchange(tokens[send_rows])
    got_up = comm.gather(my_half(up_weight))
    got_down = comm.gather(my_half(down_weight))
    arrived_grad = exchange(cotangent[send_rows])

    rows_shard = query_weight.shape[0]
    query_mat, key_mat, value_mat, out_mat, vec_all = assemble(
        pos,
        squares + (jnp.concatenate([packed, packed]),),
        got_square,
        [rows_shard] * 4 + [2 * VEC_ROWS],
        [rows_shard // 2] * 4 + [VEC_ROWS],
    )
    (up_mat,) = assemble(pos, (up_weight,), got_up, [rows_shard], [rows_shard // 2])
    down_rows = down_weight.shape[0]
    (down_mat,) = assemble(pos, (down_weight,), got_down, [down_rows], [down_rows // 2])
    vec_flat = vec_all.reshape(S, 2, VEC_ROWS * width)[:, 0]
    full_vectors = []
    at = 0
    for size in sizes:
        full_vectors.append(vec_flat[:, at : at + size].reshape(-1).astype(F32))
        at += size
    (
        query_add,
        value_add,
        out_add,
        up_add,
        down_add,
        gain_one,
        shift_one,
        gain_two,
        shift_two,
    ) = full_vectors

    inputs = arrived[pack_rows]
    grad_result = arrived_grad[pack_rows].astype(F32)
    scaling = HEAD_DIM ** (-0.5)
    head_shape = (row_count, HEADS, HEAD_DIM)
    queries = (project(inputs, query_mat) + query_add).astype(BF).reshape(head_shape)
    key_rows = project(inputs, key_mat).astype(BF).reshape(head_shape)
    value_rows = (project(inputs, value_mat) + value_add).astype(BF).reshape(head_shape)
    attended, log_sums = attend(queries, key_rows, value_rows, segments, scaling)
    attended = attended.reshape(row_count, -1)
    first_sum = inputs.astype(F32) + (project(attended, out_mat) + out_add)
    first_normed, first_spread = normalize(first_sum)
    normed_one = (first_normed * gain_one + shift_one).astype(BF)
    pre_act = project(normed_one, up_mat) + up_add
    activated = jax.nn.gelu(pre_act, approximate=False).astype(BF)
    second_sum = normed_one.astype(F32) + (project(activated, down_mat) + down_add)
    second_normed, second_spread = normalize(second_sum)
    layer_rows = (second_normed * gain_two + shift_two).astype(BF)
    inverse_pack = inverse(pack_rows)
    inverse_send = inverse(send_rows)
    layer_back = exchange(layer_rows[inverse_pack])[inverse_send]

    def split(grad):
        low = grad.astype(BF)
        rows = low.shape[0] // (2 * S)
        halves = low.reshape(S, 2, rows, low.shape[1])
        mine = lax.dynamic_index_in_dim(halves, c, 1, keepdims=False)
        theirs = lax.dynamic_index_in_dim(halves, 1 - c, 1, keepdims=False)
        return mine, theirs

    grad_gain_two = jnp.sum(grad_result * second_normed, 0)
    grad_shift_two = jnp.sum(grad_result, 0)
    grad_second = norm_back(grad_result * gain_two, second_normed, second_spread)
    grad_ffn = grad_second.astype(BF)
    grad_down = outer_sum(activated, grad_ffn)
    done_down = comm.reduce(*split(grad_down), s)
    grad_down_add = jnp.sum(grad_ffn.astype(F32), 0)
    gelu_slope = (
        0.5 * (1.0 + lax.erf(pre_act * inv_root_two))
        + pre_act * jnp.exp(-0.5 * pre_act * pre_act) * inv_root_tau
    )
    grad_pre = (project_back(grad_ffn, down_mat) * gelu_slope).astype(BF)
    grad_up = outer_sum(normed_one, grad_pre)
    done_up = comm.reduce(*split(grad_up), s)
    grad_up_add = jnp.sum(grad_pre.astype(F32), 0)
    grad_normed = grad_second + project_back(grad_pre, up_mat)
    grad_gain_one = jnp.sum(grad_normed * first_normed, 0)
    grad_shift_one = jnp.sum(grad_normed, 0)
    grad_first = norm_back(grad_normed * gain_one, first_normed, first_spread)
    grad_branch = grad_first.astype(BF)
    grad_out = outer_sum(attended, grad_branch)
    grad_out_add = jnp.sum(grad_branch.astype(F32), 0)
    grad_attended = project_back(grad_branch, out_mat).astype(BF).reshape(head_shape)
    grad_query_heads, grad_key_heads, grad_value_heads = attend_back(
        queries, key_rows, value_rows, segments, log_sums, grad_attended, scaling
    )
    grad_queries = grad_query_heads.reshape(row_count, -1).astype(BF)
    grad_keys = grad_key_heads.reshape(row_count, -1).astype(BF)
    grad_values = grad_value_heads.reshape(row_count, -1).astype(BF)
    grad_inputs = (
        grad_first
        + project_back(grad_queries, query_mat)
        + project_back(grad_keys, key_mat)
        + project_back(grad_values, value_mat)
    )
    grad_back = exchange(grad_inputs.astype(BF)[inverse_pack])[inverse_send]
    grad_query = outer_sum(inputs, grad_queries)
    grad_key = outer_sum(inputs, grad_keys)
    grad_value = outer_sum(inputs, grad_values)
    grad_query_add = jnp.sum(grad_queries.astype(F32), 0)
    grad_value_add = jnp.sum(grad_values.astype(F32), 0)
    small = [
        grad_query_add,
        grad_value_add,
        grad_out_add,
        grad_up_add,
        grad_down_add,
        grad_gain_one,
        grad_shift_one,
        grad_gain_two,
        grad_shift_two,
    ]
    small_rows = jnp.concatenate([v.reshape(S, -1) for v in small], 1)
    small_rows = jnp.pad(small_rows, ((0, 0), (0, VEC_ROWS * width - small_rows.shape[1])))
    small_rows = small_rows.reshape(S, VEC_ROWS, width).astype(BF)
    pairs = [split(g) for g in (grad_query, grad_key, grad_value, grad_out)]
    mine = jnp.concatenate([p[0] for p in pairs] + [small_rows], 1)
    theirs = jnp.concatenate([p[1] for p in pairs] + [small_rows], 1)
    done_square = comm.reduce(mine, theirs, s)

    def join(pair):
        low = jnp.where(c == 0, pair[0], pair[1])
        high = jnp.where(c == 0, pair[1], pair[0])
        return jnp.concatenate([low, high]).astype(F32)

    grads = []
    half = rows_shard // 2
    for w in range(4):
        grads.append(join([d[w * half : (w + 1) * half] for d in done_square]))
    grads.append(join(done_up))
    grads.append(join(done_down))
    flat = done_square[0][4 * half :].reshape(-1).astype(F32)
    at = 0
    for size in sizes:
        grads.append(flat[at : at + size])
        at += size
    return (layer_back, grad_back, *grads)


def solution(mesh):
    rows = P(("rep", "shard"), None)
    weight = P("shard", None)
    vector = P("shard")
    return jax.shard_map(
        functools.partial(shards, Comm(mesh)),
        mesh=mesh,
        in_specs=(rows,) * 5 + (weight,) * 6 + (vector,) * 9,
        out_specs=(rows,) * 2 + (weight,) * 6 + (vector,) * 9,
        check_vma=False,
    )
```

time: 649 us -> 427 us (0.66)
  waiting for transfers between devices: 352 us -> 124 us
  blocking collectives: 73.7 us -> 0 us
  starting transfers between devices: 20.2 us -> 79.7 us
  matrix products: 110 us -> 87.8 us
  local copies, waits for them, and re-layouts: 41.9 us -> 62 us
  other arithmetic: 29.3 us -> 48.9 us
  Pallas kernels: 0 us -> 16.1 us
  between operations: 16.8 us -> 2.19 us
    reduce_scatter x6 -> x0, waiting for transfers between devices: 149 us -> none  [the longest x1 60.1 us: shards(): lax.psum_scatter(grad_up.astype(jnp.bfloat16), 'shard', scatter_dimension...]
    all_gather x6 -> x0, waiting for transfers between devices: 135 us -> none  [the longest x1 55.8 us: shards(): lax.all_gather(up_weight, 'shard', axis=0, tiled=True)]
    ppermute x0 -> x42, waiting for transfers between devices: none -> 78.1 us  [the longest x24 75.3 us: across(): return lax.ppermute(x, 'shard', [(i, i ^ mask) for i in range(self.S)])]
    psum x1 -> x0, waiting for transfers between devices: 45.6 us -> none  [shards(): lax.psum(share_query.astype(jnp.bfloat16), 'rep').astype(jnp.float32)]
    ppermute x0 -> x42, starting transfers between devices: none -> 34.1 us  [the longest x24 30.3 us: across(): return lax.ppermute(x, 'shard', [(i, i ^ mask) for i in range(self.S)])]
    psum x1 -> x0, blocking collectives: 34.1 us -> none  [shards(): lax.psum(share_query_add.astype(jnp.bfloat16), 'rep').astype(jnp.float32)]
    unnamed x2 -> x0, blocking collectives: 32.4 us -> none
    all_to_all x4 -> x10, waiting for transfers between devices: 18.5 us -> 45.7 us  [the longest x6 45.7 us: over_z(): lax.all_to_all(x, 'rep', split_axis=0, concat_axis=0, tiled=True, axis_in...]
  transfers between devices with their start and end apart: 17 -> 52, of which waited for: 9 -> 19; matrix products, arithmetic and copies ran while one was open for 22% -> 19% of each run, Pallas kernels for 0% -> 4%
where the time goes in v1:
time: 427 us; the launch traced here: 420 us
  waiting for transfers between devices  124 us (29%)
  matrix products  87.8 us (21%)
  starting transfers between devices  79.7 us (19%)
  local copies, waits for them, and re-layouts  62 us (15%)
  other arithmetic  48.9 us (11%)
  Pallas kernels  16.1 us (4%)
    ppermute x24, waiting for transfers between devices, across(): return lax.ppermute(x, 'shard', [(i, i ^ mask) for i in range(self.S)])  75.3 us
    all_to_all x6, waiting for transfers between devices, over_z(): lax.all_to_all(x, 'rep', split_axis=0, concat_axis=0, tiled=True, axis_in...  45.7 us
    dot_general x6, matrix products, project(): return jnp.dot(left_rows, weight, preferred_element_type=F32)  30.4 us
    ppermute x24, starting transfers between devices, across(): return lax.ppermute(x, 'shard', [(i, i ^ mask) for i in range(self.S)])  30.3 us
    all_to_all x6, starting transfers between devices, over_z(): lax.all_to_all(x, 'rep', split_axis=0, concat_axis=0, tiled=True, axis_in...  24.4 us
    all_to_all x4, starting transfers between devices, exchange(): lax.all_to_all(rows, ('rep', 'shard'), split_axis=0, concat_axis=0, tiled...  21.3 us
    pallas_call x3, Pallas kernels, assemble(): pl.pallas_call(body, out_shape=[jax.ShapeDtypeStruct((S * rows, own.shape...  16.1 us
    dot_general x6, matrix products, project_back(): jnp.einsum('ti,ji->tj', left_rows, weight, preferred_element_type=F32)  14 us
  transfers between devices with their start and end apart: 52, of which 19 were waited for; matrix products, arithmetic and copies ran while one was open for 19% of the time, Pallas kernels for 4%

profile of v1, /device:TPU:0, one launch (start us, length us, event | category | flops | bytes accessed | tf_op | source)
XLA Modules:
  0.0 420.4 jit_solution(11167632729932244116)
XLA Ops:
  10.7 4.0 all-to-all-start.2
  29.1 25.5 %collective-permute-done.17.refs_2_ = bf16[384,768]{1,0:T(8,128)(2,1)} collective-permute-done((bf16[384,768]{1,0:T(8,128)(2,1)S(1)}, bf16[384,768]{1,0:T(8,128)(2,1)}, u32[]{:S(2)}, u32[]{:S(2)}) %collective-permute-start.17) | collective-permute-done | bytes 589856 | tf_op jit(solution)/shard_map/ppermute | solution.py:65
  65.2 4.3 %collective-permute-done.19.refs_4_ = bf16[192,768]{1,0:T(8,128)(2,1)} collective-permute-done((bf16[192,768]{1,0:T(8,128)(2,1)S(1)}, bf16[192,768]{1,0:T(8,128)(2,1)}, u32[]{:S(2)}, u32[]{:S(2)}) %collective-permute-start.19) | collective-permute-done | bytes 294944 | tf_op jit(solution)/shard_map/ppermute | solution.py:65
  73.6 5.7 %all-to-all-start = ((bf16[32,16,768]{2,1,0:T(8,128)(2,1)}), bf16[32,16,768]{2,1,0:T(8,128)(2,1)S(1)}, u32[]{:S(2)}, u32[]{:S(2)}) async-start(bf16[32,16,768]{2,1,0:T(8,128)(2,1)} %bitcast.2), calls=%async_computation | async-start | bytes 1572864 | tf_op jit(solution)/shard_map/all_to_all | solution.py:229
  88.5 5.1 %assemble.5 = bf16[3072,768]{1,0:T(8,128)(2,1)} custom-call(s32[2]{0:T(128)} %pad_add_fusion.pos, bf16[768,768]{1,0:T(8,128)(2,1)} %refs_0_.5, bf16[384,768]{1,0:T(8,128)(2,1)} %copy-done.16, bf16[384,768]{1,0:T(8,128)(2,1)} %collective-permute-done.17.refs_2_, bf16[192,768]{1,0:T(8,128)(2,1)} %collective-permute-done.18.refs_3_, ...), custom_call_target="tpu_custom_call" | custom-call | tf_op jit(solution)/shard_map/assemble/pallas_call | solution.py:158
  93.7 5.2 %assemble.4 = bf16[768,3072]{1,0:T(8,128)(2,1)} custom-call(s32[2]{0:T(128)} %pad_add_fusion.pos, bf16[192,3072]{1,0:T(8,128)(2,1)} %refs_0_.4, bf16[96,3072]{1,0:T(8,128)(2,1)} %collective-permute-done.8.refs_1_, bf16[96,3072]{1,0:T(8,128)(2,1)} %copy-done.15, bf16[48,3072]{1,0:T(8,128)(2,1)} %copy-done.32, ...), custom_call_target="tpu_custom_call" | custom-call | tf_op jit(solution)/shard_map/assemble/pallas_call | solution.py:158
  99.8 5.7 %assemble.3 = (bf16[768,768]{1,0:T(8,128)(2,1)}, bf16[768,768]{1,0:T(8,128)(2,1)}, bf16[768,768]{1,0:T(8,128)(2,1)}, bf16[768,768]{1,0:T(8,128)(2,1)}, bf16[256,768]{1,0:T(8,128)(2,1)}) custom-call(s32[2]{0:T(128)} %pad_add_fusion.pos, bf16[192,768]{1,0:T(8,128)(2,1)} %refs_0_.3, bf16[192,768]{1,0:T(8,128)(2,1)} %refs_1_.1, bf16[192,768]{1,0:T(8,128)(2,1)} %refs_2_.1, ...), custom_call_target="tpu_custom_call" | custom-call | tf_op jit(solution)/shard_map/assemble/pallas_call | solution.py:158
  118.0 3.5 convolution_convert_fusion.7
  129.6 4.0 fusion.35
  134.9 18.6 %fusion.4 = (bf16[512,3072]{1,0:T(8,128)(2,1)S(1)}, f32[512,3072]{1,0:T(8,128)S(1)}) fusion(f32[3072]{0:T(1024)S(1)} %reshape.444, bf16[768,3072]{1,0:T(8,128)(2,1)} %assemble.4, f32[512,768]{1,0:T(8,128)S(1)} %get-tuple-element.99, f32[768]{0:T(1024)S(1)} %reshape.443, f32[768]{0:T(1024)S(1)} %reshape.442, f32[512]{0:T(512)S(1)} %add_rsqrt_fusion.1, ...), kind=kOutput, calls=%fused_computation.22 | convolution fusion | flops 2521694208 | bytes 15751168 | tf_op jit(solution)/shard_map/dot_general | solution.py:24
  158.3 5.2 %fusion.72 = (bf16[3072]{0:T(1024)(128)(2,1)S(1)}, bf16[512,3072]{1,0:T(8,128)(2,1)S(1)}) fusion(f32[512,3072]{1,0:T(8,128)S(1)} %get-tuple-element.101, f32[3072]{0:T(1024)S(1)} %reshape.444, bf16[3072,768]{1,0:T(8,128)(2,1)S(1)} %bitcast.229, f32[512,768]{1,0:T(8,128)S(1)} %get-tuple-element.35), kind=kOutput, calls=%fused_computation.240 | convolution fusion | flops 2435183616 | bytes 15747072 | tf_op jit(solution)/shard_map/ti,ji->tj/dot_general | solution.py:28
  166.7 4.8 %convolution_convert_fusion.1 = bf16[768,3072]{1,0:T(8,128)(2,1)} fusion(bf16[512,3072]{1,0:T(8,128)(2,1)S(1)} %get-tuple-element.112, f32[512,768]{1,0:T(8,128)S(1)} %get-tuple-element.99, f32[768]{0:T(1024)S(1)} %reshape.443, f32[768]{0:T(1024)S(1)} %reshape.442, f32[512]{0:T(512)S(1)} %add_rsqrt_fusion.1, f32[512]{0:T(512)S(1)} %broadcast_multiply_fusion.5), kind=kOutput, calls=%fused_computation.49 | convolution fusion | flops 2420244480 | bytes 9447424 | tf_op jit(solution)/shard_map/ti,tj->ij/dot_general | solution.py:32
  171.5 4.4 %convolution_convert_fusion = bf16[3072,768]{1,0:T(8,128)(2,1)} fusion(bf16[512,3072]{1,0:T(8,128)(2,1)S(1)} %get-tuple-element.100, f32[512,768]{1,0:T(8,128)S(1)} %get-tuple-element.35), kind=kOutput, calls=%fused_computation.48 | convolution fusion | flops 2418671616 | bytes 9437184 | tf_op jit(solution)/shard_map/ti,tj->ij/dot_general | solution.py:32
  180.4 9.0 %fusion.71 = (bf16[12,64]{1,0:T(8,128)(2,1)S(1)}, bf16[12,64,512]{2,1,0:T(8,128)(2,1)}) fusion(bf16[512,12,64]{0,2,1:T(8,128)(2,1)} %bitcast.234, f32[12,512]{1,0:T(8,128)S(1)} %log_add_fusion, f32[12,512,512]{1,2,0:T(8,128)} %copy-done.2, pred[512,512]{0,1:T(8,128)(4,1)S(1)} %broadcast_compare_fusion), kind=kOutput, calls=%fused_computation.239 | convolution fusion | flops 416021760 | bytes 14444032 | tf_op jit(solution)/shard_map/hqk,qhd->khd/dot_general | solution.py:198
  189.4 9.6 %multiply_reduce_fusion = (f32[12,512]{1,0:T(8,128)S(1)}, f32[12,512,512]{1,2,0:T(8,128)}) fusion(f32[12,512]{1,0:T(8,128)S(1)} %log_add_fusion, f32[12,512,512]{1,2,0:T(8,128)} %copy-done.2, pred[512,512]{0,1:T(8,128)(4,1)S(1)} %broadcast_compare_fusion, bf16[512,12,64]{0,2,1:T(8,128)(2,1)S(1)} %bitcast.235, bf16[512,12,64]{0,2,1:T(8,128)(2,1)S(1)} %bitcast.233), kind=kOutput, calls=%fused_computation.11 | convolution fusion | flops 418375680 | bytes 27049984 | tf_op jit(solution)/shard_map/qhd,khd->hqk/dot_general | solution.py:189
  199.0 7.2 %multiply_convert_fusion = bf16[12,512,512]{1,2,0:T(8,128)(2,1)S(1)} fusion(f32[12,512,512]{1,2,0:T(8,128)} %get-tuple-element.106, f32[12,512]{1,0:T(8,128)S(1)} %get-tuple-element.105, f32[12,512]{1,0:T(8,128)S(1)} %log_add_fusion, f32[12,512,512]{1,2,0:T(8,128)S(1)} %bitcast.210, pred[512,512]{0,1:T(8,128)(4,1)S(1)} %broadcast_compare_fusion), kind=kLoop, calls=%fused_computation.10 | loop fusion | flops 18874368 | bytes 31768576 | tf_op jit(solution)/shard_map/convert_element_type | solution.py:191
  214.3 5.7 %all-to-all-start.1 = ((bf16[32,16,768]{2,1,0:T(8,128)(2,1)}), bf16[32,16,768]{2,1,0:T(8,128)(2,1)S(1)}, u32[]{:S(2)}, u32[]{:S(2)}) async-start(bf16[32,16,768]{2,1,0:T(8,128)(2,1)} %bitcast.236), calls=%async_computation.1 | async-start | bytes 1572864 | tf_op jit(solution)/shard_map/all_to_all | solution.py:229
  252.3 9.7 %collective-permute-done.31 = bf16[96,3072]{1,0:T(8,128)(2,1)S(1)} collective-permute-done((bf16[96,3072]{1,0:T(8,128)(2,1)S(1)}, bf16[96,3072]{1,0:T(8,128)(2,1)S(1)}, u32[]{:S(2)}, u32[]{:S(2)}) %collective-permute-start.31) | collective-permute-done | bytes 589856 | tf_op jit(solution)/shard_map/ppermute | solution.py:65
  265.3 5.8 %all-to-all-start.3 = ((bf16[32,16,768]{2,1,0:T(8,128)(2,1)}), bf16[32,16,768]{2,1,0:T(8,128)(2,1)S(1)}, u32[]{:S(2)}, u32[]{:S(2)}) async-start(bf16[32,16,768]{2,1,0:T(8,128)(2,1)} %bitcast.26), calls=%async_computation.3 | async-start | bytes 1572864 | tf_op jit(solution)/shard_map/all_to_all | solution.py:229
  271.1 13.2 %collective-permute-done.32 = bf16[48,3072]{1,0:T(8,128)(2,1)} collective-permute-done((bf16[48,3072]{1,0:T(8,128)(2,1)}, bf16[48,3072]{1,0:T(8,128)(2,1)}, u32[]{:S(2)}, u32[]{:S(2)}) %collective-permute-start.32) | collective-permute-done | bytes 294944 | tf_op jit(solution)/shard_map/ppermute | solution.py:65
  292.9 3.8 collective-permute-done.34
  298.7 4.7 %all-to-all-start.6 = ((bf16[4,24,3072]{2,1,0:T(8,128)(2,1)}), bf16[4,24,3072]{2,1,0:T(8,128)(2,1)S(1)}, u32[]{:S(2)}, u32[]{:S(2)}) async-start(bf16[4,24,3072]{2,1,0:T(8,128)(2,1)} %bitcast.65), calls=%async_computation.6 | async-start | bytes 1179648 | tf_op jit(solution)/shard_map/all_to_all | solution.py:71
  316.8 4.5 %all-to-all-start.8 = ((bf16[4,96,768]{2,1,0:T(8,128)(2,1)}), bf16[4,96,768]{2,1,0:T(8,128)(2,1)S(1)}, u32[]{:S(2)}, u32[]{:S(2)}) async-start(bf16[4,96,768]{2,1,0:T(8,128)(2,1)} %bitcast.78), calls=%async_computation.8 | async-start | bytes 1179648 | tf_op jit(solution)/shard_map/all_to_all | solution.py:71
  328.6 6.6 %collective-permute-done.28 = bf16[208,768]{1,0:T(8,128)(2,1)S(1)} collective-permute-done((bf16[208,768]{1,0:T(8,128)(2,1)S(1)}, bf16[208,768]{1,0:T(8,128)(2,1)S(1)}, u32[]{:S(2)}, u32[]{:S(2)}) %collective-permute-start.28) | collective-permute-done | bytes 319520 | tf_op jit(solution)/shard_map/ppermute | solution.py:65
  337.2 4.8 %all-to-all-start.4 = ((bf16[4,104,768]{2,1,0:T(8,128)(2,1)}), bf16[4,104,768]{2,1,0:T(8,128)(2,1)S(1)}, u32[]{:S(2)}, u32[]{:S(2)}) async-start(bf16[4,104,768]{2,1,0:T(8,128)(2,1)} %bitcast.52), calls=%async_computation.4 | async-start | bytes 1277952 | tf_op jit(solution)/shard_map/all_to_all | solution.py:71
  342.1 13.2 %all-to-all-done.4 = bf16[4,104,768]{2,1,0:T(8,128)(2,1)S(1)} async-done(((bf16[4,104,768]{2,1,0:T(8,128)(2,1)}), bf16[4,104,768]{2,1,0:T(8,128)(2,1)S(1)}, u32[]{:S(2)}, u32[]{:S(2)}) %all-to-all-start.4) | async-done | bytes 639008 | tf_op jit(solution)/shard_map/all_to_all | solution.py:71
  356.2 3.5 all-to-all-start.7
  359.8 13.2 %all-to-all-done.7 = bf16[4,24,3072]{2,1,0:T(8,128)(2,1)S(1)} async-done(((bf16[4,24,3072]{2,1,0:T(8,128)(2,1)}), bf16[4,24,3072]{2,1,0:T(8,128)(2,1)S(1)}, u32[]{:S(2)}, u32[]{:S(2)}) %all-to-all-start.7) | async-done | bytes 589856 | tf_op jit(solution)/shard_map/all_to_all | solution.py:71
  373.8 3.5 all-to-all-start.9
  377.4 13.4 %all-to-all-done.9 = bf16[4,96,768]{2,1,0:T(8,128)(2,1)S(1)} async-done(((bf16[4,96,768]{2,1,0:T(8,128)(2,1)}), bf16[4,96,768]{2,1,0:T(8,128)(2,1)S(1)}, u32[]{:S(2)}, u32[]{:S(2)}) %all-to-all-start.9) | async-done | bytes 589856 | tf_op jit(solution)/shard_map/all_to_all | solution.py:71
  391.7 3.5 all-to-all-start.5
  403.7 5.9 %all-to-all-done.5 = bf16[4,104,768]{2,1,0:T(8,128)(2,1)S(1)} async-done(((bf16[4,104,768]{2,1,0:T(8,128)(2,1)}), bf16[4,104,768]{2,1,0:T(8,128)(2,1)S(1)}, u32[]{:S(2)}, u32[]{:S(2)}) %all-to-all-start.5) | async-done | bytes 639008 | tf_op jit(solution)/shard_map/all_to_all | solution.py:71
  (352 shorter events, 181.7 us)
Async XLA Ops:
  2.7 21.4 %collective-permute-start.9 = (bf16[96,3072]{1,0:T(8,128)(2,1)}, bf16[96,3072]{1,0:T(8,128)(2,1)S(1)}, u32[]{:S(2)}, u32[]{:S(2)}) collective-permute-start(bf16[96,3072]{1,0:T(8,128)(2,1)} %constant_dynamic-slice_fusion.1), channel_id=1, source_target_pairs={{0,2},{1,3},{2,0},{3,1},{4,6},{5,7},{6,4},{7,5},{8,10},{9,11},{10,... | collective-permute-start | bytes 1769480 | tf_op jit(solution)/shard_map/ppermute | solution.py:65
  5.6 20.2 %collective-permute-start.8 = (bf16[96,3072]{1,0:T(8,128)(2,1)}, bf16[96,3072]{1,0:T(8,128)(2,1)}, u32[]{:S(2)}, u32[]{:S(2)}) collective-permute-start(bf16[96,3072]{1,0:T(8,128)(2,1)} %constant_dynamic-slice_fusion.1), channel_id=1, source_target_pairs={{0,1},{1,0},{2,3},{3,2},{4,5},{5,4},{6,7},{7,6},{8,9},{9,8},{10,11... | collective-permute-start | bytes 1769480 | tf_op jit(solution)/shard_map/ppermute | solution.py:65
  10.7 62.9 %all-to-all-start.2 = ((bf16[32,16,768]{2,1,0:T(8,128)(2,1)}), bf16[32,16,768]{2,1,0:T(8,128)(2,1)S(1)}, u32[]{:S(2)}, u32[]{:S(2)}) async-start(bf16[32,16,768]{2,1,0:T(8,128)(2,1)} %bitcast.17), calls=%async_computation.2 | async-start | bytes 1572864 | tf_op jit(solution)/shard_map/all_to_all | solution.py:229
  20.2 38.2 %collective-permute-start.1 = (bf16[416,768]{1,0:T(8,128)(2,1)}, bf16[416,768]{1,0:T(8,128)(2,1)}, u32[]{:S(2)}, u32[]{:S(2)}) collective-permute-start(bf16[416,768]{1,0:T(8,128)(2,1)} %constant_dynamic-update-slice_fusion), channel_id=1, source_target_pairs={{0,2},{1,3},{2,0},{3,1},{4,6},{5,7},{6,4},{7,5},{8,10},{9,11},{10,... | collective-permute-start | bytes 1916936 | tf_op jit(solution)/shard_map/ppermute | solution.py:65
  22.0 32.6 %collective-permute-start.17 = (bf16[384,768]{1,0:T(8,128)(2,1)S(1)}, bf16[384,768]{1,0:T(8,128)(2,1)}, u32[]{:S(2)}, u32[]{:S(2)}) collective-permute-start(bf16[384,768]{1,0:T(8,128)(2,1)S(1)} %constant_dynamic-slice_fusion), channel_id=1, source_target_pairs={{0,2},{1,3},{2,0},{3,1},{4,6},{5,7},{6,4},{7,5},{8,10},{9,11},{10,... | collective-permute-start | bytes 1769480 | tf_op jit(solution)/shard_map/ppermute | solution.py:65
  22.3 34.5 %collective-permute-start.16 = (bf16[384,768]{1,0:T(8,128)(2,1)S(1)}, bf16[384,768]{1,0:T(8,128)(2,1)S(1)}, u32[]{:S(2)}, u32[]{:S(2)}) collective-permute-start(bf16[384,768]{1,0:T(8,128)(2,1)S(1)} %constant_dynamic-slice_fusion), channel_id=1, source_target_pairs={{0,1},{1,0},{2,3},{3,2},{4,5},{5,4},{6,7},{7,6},{8,9},{9,8},{10,11... | collective-permute-start | bytes 1769480 | tf_op jit(solution)/shard_map/ppermute | solution.py:65
  24.1 35.9 %collective-permute-start = (bf16[416,768]{1,0:T(8,128)(2,1)}, bf16[416,768]{1,0:T(8,128)(2,1)S(1)}, u32[]{:S(2)}, u32[]{:S(2)}) collective-permute-start(bf16[416,768]{1,0:T(8,128)(2,1)} %constant_dynamic-update-slice_fusion), channel_id=1, source_target_pairs={{0,1},{1,0},{2,3},{3,2},{4,5},{5,4},{6,7},{7,6},{8,9},{9,8},{10,11... | collective-permute-start | bytes 1916936 | tf_op jit(solution)/shard_map/ppermute | solution.py:65
  25.8 37.3 %collective-permute-start.11 = (bf16[48,3072]{1,0:T(8,128)(2,1)S(1)}, bf16[48,3072]{1,0:T(8,128)(2,1)}, u32[]{:S(2)}, u32[]{:S(2)}) collective-permute-start(bf16[48,3072]{1,0:T(8,128)(2,1)S(1)} %slice.365), channel_id=1, source_target_pairs={{0,1},{1,0},{2,3},{3,2},{4,5},{5,4},{6,7},{7,6},{8,9},{9,8},{10,11... | collective-permute-start | bytes 884744 | tf_op jit(solution)/shard_map/ppermute | solution.py:65
  60.0 19.4 %collective-permute-start.3 = (bf16[208,768]{1,0:T(8,128)(2,1)S(1)}, bf16[208,768]{1,0:T(8,128)(2,1)}, u32[]{:S(2)}, u32[]{:S(2)}) collective-permute-start(bf16[208,768]{1,0:T(8,128)(2,1)S(1)} %slice.357), channel_id=1, source_target_pairs={{0,1},{1,0},{2,3},{3,2},{4,5},{5,4},{6,7},{7,6},{8,9},{9,8},{10,11... | collective-permute-start | bytes 958472 | tf_op jit(solution)/shard_map/ppermute | solution.py:65
  63.2 16.5 %collective-permute-start.2 = (bf16[208,768]{1,0:T(8,128)(2,1)}, bf16[208,768]{1,0:T(8,128)(2,1)}, u32[]{:S(2)}, u32[]{:S(2)}) collective-permute-start(bf16[208,768]{1,0:T(8,128)(2,1)} %slice.356), channel_id=1, source_target_pairs={{0,2},{1,3},{2,0},{3,1},{4,6},{5,7},{6,4},{7,5},{8,10},{9,11},{10,... | collective-permute-start | bytes 958472 | tf_op jit(solution)/shard_map/ppermute | solution.py:65
  65.2 17.4 %collective-permute-start.13 = (bf16[96,3072]{1,0:T(8,128)(2,1)S(1)}, bf16[96,3072]{1,0:T(8,128)(2,1)}, u32[]{:S(2)}, u32[]{:S(2)}) collective-permute-start(bf16[96,3072]{1,0:T(8,128)(2,1)S(1)} %collective-permute-done.9.refs_2_), channel_id=1, source_target_pairs={{0,4},{4,0},{8,12},{12,8},{16,20},{20,16},{24,28},{28,24},{1,5},{5... | collective-permute-start | bytes 1769480 | tf_op jit(solution)/shard_map/ppermute | solution.py:68
  73.6 36.2 %all-to-all-start = ((bf16[32,16,768]{2,1,0:T(8,128)(2,1)}), bf16[32,16,768]{2,1,0:T(8,128)(2,1)S(1)}, u32[]{:S(2)}, u32[]{:S(2)}) async-start(bf16[32,16,768]{2,1,0:T(8,128)(2,1)} %bitcast.2), calls=%async_computation | async-start | bytes 1572864 | tf_op jit(solution)/shard_map/all_to_all | solution.py:229
  83.0 16.0 %collective-permute-start.5 = (bf16[416,768]{1,0:T(8,128)(2,1)}, bf16[416,768]{1,0:T(8,128)(2,1)S(1)}, u32[]{:S(2)}, u32[]{:S(2)}) collective-permute-start(bf16[416,768]{1,0:T(8,128)(2,1)} %collective-permute-done.1.refs_6_), channel_id=1, source_target_pairs={{0,4},{4,0},{8,12},{12,8},{16,20},{20,16},{24,28},{28,24},{1,5},{5... | collective-permute-start | bytes 1916936 | tf_op jit(solution)/shard_map/ppermute | solution.py:68
  83.2 15.7 %collective-permute-start.4 = (bf16[416,768]{1,0:T(8,128)(2,1)S(1)}, bf16[416,768]{1,0:T(8,128)(2,1)}, u32[]{:S(2)}, u32[]{:S(2)}) collective-permute-start(bf16[416,768]{1,0:T(8,128)(2,1)S(1)} %collective-permute-done.refs_5_), channel_id=1, source_target_pairs={{0,4},{4,0},{8,12},{12,8},{16,20},{20,16},{24,28},{28,24},{1,5},{5... | collective-permute-start | bytes 1916936 | tf_op jit(solution)/shard_map/ppermute | solution.py:68
  214.3 51.0 %all-to-all-start.1 = ((bf16[32,16,768]{2,1,0:T(8,128)(2,1)}), bf16[32,16,768]{2,1,0:T(8,128)(2,1)S(1)}, u32[]{:S(2)}, u32[]{:S(2)}) async-start(bf16[32,16,768]{2,1,0:T(8,128)(2,1)} %bitcast.236), calls=%async_computation.1 | async-start | bytes 1572864 | tf_op jit(solution)/shard_map/all_to_all | solution.py:229
  226.9 20.3 %collective-permute-start.36 = (bf16[4,384,768]{2,1,0:T(8,128)(2,1)}, bf16[4,384,768]{2,1,0:T(8,128)(2,1)}, u32[]{:S(2)}, u32[]{:S(2)}) collective-permute-start(bf16[4,384,768]{2,1,0:T(8,128)(2,1)} %dynamic-slice_bitcast_fusion), channel_id=1, source_target_pairs={{0,4},{4,0},{8,12},{12,8},{16,20},{20,16},{24,28},{28,24},{1,5},{5... | collective-permute-start | bytes 7077896 | tf_op jit(solution)/shard_map/ppermute | solution.py:68
  240.3 22.8 %collective-permute-start.24 = (bf16[4,416,768]{2,1,0:T(8,128)(2,1)S(1)}, bf16[4,416,768]{2,1,0:T(8,128)(2,1)S(1)}, u32[]{:S(2)}, u32[]{:S(2)}) collective-permute-start(bf16[4,416,768]{2,1,0:T(8,128)(2,1)S(1)} %get-tuple-element.79), channel_id=1, source_target_pairs={{0,4},{4,0},{8,12},{12,8},{16,20},{20,16},{24,28},{28,24},{1,5},{5... | collective-permute-start | bytes 7667720 | tf_op jit(solution)/shard_map/ppermute | solution.py:68
  243.8 27.3 %collective-permute-start.33 = (bf16[96,3072]{1,0:T(8,128)(2,1)S(1)}, bf16[96,3072]{1,0:T(8,128)(2,1)}, u32[]{:S(2)}, u32[]{:S(2)}) collective-permute-start(bf16[96,3072]{1,0:T(8,128)(2,1)S(1)} %pad_maximum_fusion.4), channel_id=1, source_target_pairs={{0,2},{1,3},{2,0},{3,1},{4,6},{5,7},{6,4},{7,5},{8,10},{9,11},{10,... | collective-permute-start | bytes 1769480 | tf_op jit(solution)/shard_map/ppermute | solution.py:65
  245.7 16.3 %collective-permute-start.31 = (bf16[96,3072]{1,0:T(8,128)(2,1)S(1)}, bf16[96,3072]{1,0:T(8,128)(2,1)S(1)}, u32[]{:S(2)}, u32[]{:S(2)}) collective-permute-start(bf16[96,3072]{1,0:T(8,128)(2,1)S(1)} %pad_maximum_fusion.3), channel_id=1, source_target_pairs={{0,1},{1,0},{2,3},{3,2},{4,5},{5,4},{6,7},{7,6},{8,9},{9,8},{10,11... | collective-permute-start | bytes 1769480 | tf_op jit(solution)/shard_map/ppermute | solution.py:65
  250.6 52.8 %collective-permute-start.39 = (bf16[384,768]{1,0:T(8,128)(2,1)}, bf16[384,768]{1,0:T(8,128)(2,1)}, u32[]{:S(2)}, u32[]{:S(2)}) collective-permute-start(bf16[384,768]{1,0:T(8,128)(2,1)} %pad_maximum_fusion.7), channel_id=1, source_target_pairs={{0,2},{1,3},{2,0},{3,1},{4,6},{5,7},{6,4},{7,5},{8,10},{9,11},{10,... | collective-permute-start | bytes 1769480 | tf_op jit(solution)/shard_map/ppermute | solution.py:65
  252.0 36.9 %collective-permute-start.37 = (bf16[384,768]{1,0:T(8,128)(2,1)}, bf16[384,768]{1,0:T(8,128)(2,1)}, u32[]{:S(2)}, u32[]{:S(2)}) collective-permute-start(bf16[384,768]{1,0:T(8,128)(2,1)} %pad_maximum_fusion.6), channel_id=1, source_target_pairs={{0,1},{1,0},{2,3},{3,2},{4,5},{5,4},{6,7},{7,6},{8,9},{9,8},{10,11... | collective-permute-start | bytes 1769480 | tf_op jit(solution)/shard_map/ppermute | solution.py:65
  262.9 21.4 %collective-permute-start.32 = (bf16[48,3072]{1,0:T(8,128)(2,1)}, bf16[48,3072]{1,0:T(8,128)(2,1)}, u32[]{:S(2)}, u32[]{:S(2)}) collective-permute-start(bf16[48,3072]{1,0:T(8,128)(2,1)} %fusion.51), channel_id=1, source_target_pairs={{0,2},{1,3},{2,0},{3,1},{4,6},{5,7},{6,4},{7,5},{8,10},{9,11},{10,... | collective-permute-start | bytes 884744 | tf_op jit(solution)/shard_map/ppermute | solution.py:65
  265.3 33.4 %all-to-all-start.3 = ((bf16[32,16,768]{2,1,0:T(8,128)(2,1)}), bf16[32,16,768]{2,1,0:T(8,128)(2,1)S(1)}, u32[]{:S(2)}, u32[]{:S(2)}) async-start(bf16[32,16,768]{2,1,0:T(8,128)(2,1)} %bitcast.26), calls=%async_computation.3 | async-start | bytes 1572864 | tf_op jit(solution)/shard_map/all_to_all | solution.py:229
  288.9 21.5 %collective-permute-start.25 = (bf16[416,768]{1,0:T(8,128)(2,1)}, bf16[416,768]{1,0:T(8,128)(2,1)S(1)}, u32[]{:S(2)}, u32[]{:S(2)}) collective-permute-start(bf16[416,768]{1,0:T(8,128)(2,1)} %pad_maximum_fusion), channel_id=1, source_target_pairs={{0,1},{1,0},{2,3},{3,2},{4,5},{5,4},{6,7},{7,6},{8,9},{9,8},{10,11... | collective-permute-start | bytes 1916936 | tf_op jit(solution)/shard_map/ppermute | solution.py:65
  298.7 18.2 %all-to-all-start.6 = ((bf16[4,24,3072]{2,1,0:T(8,128)(2,1)}), bf16[4,24,3072]{2,1,0:T(8,128)(2,1)S(1)}, u32[]{:S(2)}, u32[]{:S(2)}) async-start(bf16[4,24,3072]{2,1,0:T(8,128)(2,1)} %bitcast.65), calls=%async_computation.6 | async-start | bytes 1179648 | tf_op jit(solution)/shard_map/all_to_all | solution.py:71
  307.7 15.6 %collective-permute-start.27 = (bf16[416,768]{1,0:T(8,128)(2,1)}, bf16[416,768]{1,0:T(8,128)(2,1)}, u32[]{:S(2)}, u32[]{:S(2)}) collective-permute-start(bf16[416,768]{1,0:T(8,128)(2,1)} %pad_maximum_fusion.1), channel_id=1, source_target_pairs={{0,2},{1,3},{2,0},{3,1},{4,6},{5,7},{6,4},{7,5},{8,10},{9,11},{10,... | collective-permute-start | bytes 1916936 | tf_op jit(solution)/shard_map/ppermute | solution.py:65
  312.3 14.3 %collective-permute-start.26 = (bf16[208,768]{1,0:T(8,128)(2,1)}, bf16[208,768]{1,0:T(8,128)(2,1)S(1)}, u32[]{:S(2)}, u32[]{:S(2)}) collective-permute-start(bf16[208,768]{1,0:T(8,128)(2,1)} %fusion.39), channel_id=1, source_target_pairs={{0,2},{1,3},{2,0},{3,1},{4,6},{5,7},{6,4},{7,5},{8,10},{9,11},{10,... | collective-permute-start | bytes 958472 | tf_op jit(solution)/shard_map/ppermute | solution.py:65
  316.8 20.4 %all-to-all-start.8 = ((bf16[4,96,768]{2,1,0:T(8,128)(2,1)}), bf16[4,96,768]{2,1,0:T(8,128)(2,1)S(1)}, u32[]{:S(2)}, u32[]{:S(2)}) async-start(bf16[4,96,768]{2,1,0:T(8,128)(2,1)} %bitcast.78), calls=%async_computation.8 | async-start | bytes 1179648 | tf_op jit(solution)/shard_map/all_to_all | solution.py:71
  337.2 18.1 %all-to-all-start.4 = ((bf16[4,104,768]{2,1,0:T(8,128)(2,1)}), bf16[4,104,768]{2,1,0:T(8,128)(2,1)S(1)}, u32[]{:S(2)}, u32[]{:S(2)}) async-start(bf16[4,104,768]{2,1,0:T(8,128)(2,1)} %bitcast.52), calls=%async_computation.4 | async-start | bytes 1277952 | tf_op jit(solution)/shard_map/all_to_all | solution.py:71
  356.2 16.8 %all-to-all-start.7 = ((bf16[4,24,3072]{2,1,0:T(8,128)(2,1)}), bf16[4,24,3072]{2,1,0:T(8,128)(2,1)S(1)}, u32[]{:S(2)}, u32[]{:S(2)}) async-start(bf16[4,24,3072]{2,1,0:T(8,128)(2,1)} %broadcast_in_dim.31), calls=%async_computation.7 | async-start | bytes 1179648 | tf_op jit(solution)/shard_map/all_to_all | solution.py:71
  373.8 17.0 %all-to-all-start.9 = ((bf16[4,96,768]{2,1,0:T(8,128)(2,1)}), bf16[4,96,768]{2,1,0:T(8,128)(2,1)S(1)}, u32[]{:S(2)}, u32[]{:S(2)}) async-start(bf16[4,96,768]{2,1,0:T(8,128)(2,1)} %broadcast_in_dim.32), calls=%async_computation.9 | async-start | bytes 1179648 | tf_op jit(solution)/shard_map/all_to_all | solution.py:71
  391.7 18.0 %all-to-all-start.5 = ((bf16[4,104,768]{2,1,0:T(8,128)(2,1)}), bf16[4,104,768]{2,1,0:T(8,128)(2,1)S(1)}, u32[]{:S(2)}, u32[]{:S(2)}) async-start(bf16[4,104,768]{2,1,0:T(8,128)(2,1)} %broadcast_in_dim.30), calls=%async_computation.5 | async-start | bytes 1277952 | tf_op jit(solution)/shard_map/all_to_all | solution.py:71
  (78 other events, 715.7 us)
